TPU v7x, 32 devices: a whole 2x2x4 slice. The times are simulated.
32 devices in a mesh: gx: 2 (over x), gy: 16 (over z, y, core).
Axes of the slice: x: 2, y: 2, z: 4, core: 2. Of those that a mesh axis runs over, the one named last changes fastest.
Arguments:
- residual_in: float32 [2, 16, 1024, 256], P('gx', 'gy'), may hold values from -6 to 6
- neumann: float32 [2, 16, 1024, 1024], P('gx', 'gy'), may hold values from -0.1875 to 0.1875
- dirichlet: float32 [2, 16, 1024, 1024], P('gx', 'gy'), may hold values from -0.1875 to 0.1875
- coarse: float32 [2, 1024, 1024], P('gx', 'gy'), may hold values from -0.1875 to 0.1875
- decay: float32 [2, 16, 64], P('gx', 'gy'), may hold values from 0.4 to 1
- face_rows: int32 [2, 16, 1024], P('gx', 'gy'), may hold values from 0 to 1023, each once within a row
- primal: int32 [2, 16, 64], P('gx', 'gy'), may hold values from 0 to 1023, as said below
Outputs:
- solution: float32 [2, 16, 1024, 256], P('gx', 'gy')
- residual: float32 [2, 16, 1024, 256], P('gx', 'gy')
Inputs may be any that keep to these rules, and one draw needn't show every extreme that they name: `primal`: each subdomain's 64 entries are distinct rows of its interface. `face_rows`: each subdomain's entries name every interface row once.
All inputs are finite; a program needn't handle non-finite values.
Results may differ from a plain program's by a relative error of at most 0.0001.
Values sent between devices are 32-bit elements; how exact they have to be, the bound alone decides.
A program may use at most 64 MiB of HBM per device.

v0:
```python
import functools

import jax
import jax.numpy as jnp
from jax import lax
from jax.experimental import pallas as pl
from jax.experimental.pallas import tpu as pltpu
from jax.sharding import PartitionSpec as P

STEPS = 2
MESH = pl.DeviceIdType.MESH
F32 = jnp.float32
BF16 = jnp.bfloat16


def dot(a, b):
    return jnp.dot(a, b, preferred_element_type=F32)


def split(x):
    high = x.astype(BF16)
    return high, (x - high.astype(F32)).astype(BF16)


def dot3(a, b):
    return dot(a[0], b[0]) + dot(a[0], b[1]) + dot(a[1], b[0])


def line_sizes(count):
    chips = count // 2
    inner = 1
    while inner * inner * 4 <= chips:
        inner *= 2
    return chips // inner, inner


def kernel(
    nx, ny_all, r_hbm, n_hbm, d_hbm, c_hbm, decay_ref, rows_ref, prim_ref,
    t1_hbm, t2_hbm, deh_hbm, del_hbm, chain_ref,
    n_buf, d_buf, nh, nl, dh, dl, perm, perm_t,
    r_buf, jump, upd, sol, res, fsend, frecv, c_all, psend, gath, qsend, cown, cprev, csend,
    sel_h, sel_l, nph, npl, deh, del_, pdeh, pdel, base,
    load_sem, out_sem, cf_ssem, cp_ssem, c_rsem, f_ssem, f_rsem, a_ssem, g_rsem,
    q_ssem, q_rsem, p_ssem, p_rsem,
):
    unknowns, width = r_buf.shape
    face = unknowns // 4
    prims = c_all.shape[1]
    nz, ny = line_sizes(ny_all)
    ng = 2 * ny
    part = width // ng
    fold = max(1, 128 // part)
    short = prims // fold
    block = 2 * face
    blocks = unknowns // block

    a = lax.axis_index("gx")
    me = lax.axis_index("gy")
    g = me % ng
    z = me // ng
    core = g % 2
    y = g // 2
    partner = me + 1 - 2 * core

    def pack(x):
        return jnp.concatenate([x[j * short : (j + 1) * short] for j in range(fold)], axis=1)

    def unpack(x):
        return jnp.concatenate([x[:, j * part : (j + 1) * part] for j in range(fold)], axis=0)

    def rows_of(i, size):
        return pl.ds(pl.multiple_of(i * size, size), size)

    def remote(src, dst, send, recv, gx, gy):
        return pltpu.make_async_remote_copy(
            src_ref=src, dst_ref=dst, send_sem=send, recv_sem=recv,
            device_id=(gx, gy), device_id_type=MESH,
        )

    loads = [
        pltpu.make_async_copy(src, dst, load_sem.at[i])
        for i, (src, dst) in enumerate(
            [(r_hbm, r_buf), (c_hbm, c_all.at[g]), (n_hbm, n_buf), (d_hbm, d_buf)]
        )
    ]
    loads[0].start()

    barrier = pltpu.get_barrier_semaphore()

    def greet(gx, gy):
        pl.semaphore_signal(barrier, inc=1, device_id=(gx, gy), device_id_type=MESH)

    for d in range(1, ny_all):
        greet(a, (me + d) % ny_all)
    count = ny_all - 1
    has = [a > 0, a < nx - 1, me > 0, me < ny_all - 1]
    to = [(a - 1, me), (a + 1, me), (a, me - 1), (a, me + 1)]
    for k in range(2):
        pl.when(has[k])(functools.partial(greet, *to[k]))
        count = count + has[k].astype(jnp.int32)
    mates = [z * ng + (g + d) % ng for d in range(ng)]
    mate_at = [(g + d) % ng for d in range(ng)]
    if nx > 1:

        @pl.when(a < 2)
        def _():
            for d in range(1, ng):
                greet(1 - a, mates[d])

        count = count + (a < 2).astype(jnp.int32) * (ng - 1)

    other = [1, 0, 3, 2]

    def face_copy(step, k):
        return remote(
            fsend.at[step, pl.ds(k * face, face), :],
            frecv.at[step, pl.ds(other[k] * face, face), :],
            f_ssem.at[step, k],
            f_rsem.at[step, other[k]],
            *to[k],
        )

    def face_wait(step, k):
        face_copy(step, other[k]).wait_recv()

    lanes = 128
    rows_f = rows_ref[...].astype(F32)
    rows_t = jnp.transpose(jnp.broadcast_to(rows_f, (lanes, unknowns)))

    def build_face(k):
        low, high = k * face, (k + 1) * face
        for t in range(unknowns // lanes):
            cols = lax.broadcasted_iota(jnp.int32, (face, lanes), 1) + t * lanes
            perm[low:high, t * lanes : (t + 1) * lanes] = jnp.where(
                rows_t[low:high] == cols.astype(F32), 1.0, 0.0
            ).astype(BF16)

    def take_face(step, k, field):
        low, high = k * face, (k + 1) * face
        picks = perm[low:high, :]
        fsend[step, low:high, :] = dot(picks, field[0]) + dot(picks, field[1])

    for k in range(2):
        pl.when(has[k])(functools.partial(build_face, k))
    loads[0].wait()
    for load in loads[1:]:
        load.start()
    field = split(r_buf[...])
    pl.when(has[0])(functools.partial(take_face, 0, 0, field))
    pl.when(has[1])(functools.partial(take_face, 0, 1, field))
    pl.semaphore_wait(barrier, count)
    for k in range(2):
        pl.when(has[k])(face_copy(0, k).start)
    for k in range(2, 4):

        @pl.when(has[k])
        def _(k=k):
            build_face(k)
            take_face(0, k, field)
            face_copy(0, k).start()

    for k in range(4):
        pl.when(jnp.logical_not(has[k]))(functools.partial(build_face, k))

    def coarse_far(dy):
        return remote(
            c_all.at[g], c_all.at[g], cf_ssem.at[dy], c_rsem.at[g],
            a, z * ng + ((y + dy) % ny) * 2 + core,
        )

    def coarse_near(dy):
        which = ((y + dy) % ny) * 2 + core
        return remote(
            c_all.at[which], c_all.at[which], cp_ssem.at[dy], c_rsem.at[which], a, partner
        )

    def coarse_arrived(which):
        remote(
            c_all.at[which], c_all.at[which], cp_ssem.at[0], c_rsem.at[which], a, partner
        ).wait_recv()

    loads[1].wait()
    coarse_near(0).start()
    for dy in range(1, ny):
        coarse_far(dy).start()

    for step in range(STEPS):
        for k in range(4):

            @pl.when(jnp.logical_not(has[k]))
            def _(step=step, k=k):
                frecv[step, k * face : (k + 1) * face, :] = jnp.zeros((face, width), F32)

    def build_t(i, carry):
        at = rows_of(i, block)
        here = lax.broadcasted_iota(jnp.int32, (block, unknowns), 0) + i * block
        perm_t[at, :] = jnp.where(here.astype(F32) == rows_f, 1.0, 0.0).astype(BF16)
        return carry

    lax.fori_loop(0, blocks, build_t, 0)

    eye = lax.broadcasted_iota(jnp.int32, (prims, prims), 0) == lax.broadcasted_iota(
        jnp.int32, (prims, prims), 1
    )
    prim_row = prim_ref[...].astype(F32)
    prim_col = jnp.sum(jnp.where(eye, prim_row, 0.0), axis=1, keepdims=True)
    rate = jnp.sum(jnp.where(eye, decay_ref[...], 0.0), axis=1, keepdims=True)
    pick_t = jnp.where(
        prim_col == lax.broadcasted_iota(jnp.int32, (prims, unknowns), 1).astype(F32), 1.0, 0.0
    ).astype(BF16)
    pick = jnp.where(
        lax.broadcasted_iota(jnp.int32, (unknowns, prims), 0).astype(F32) == prim_row, 1.0, 0.0
    ).astype(BF16)

    def halves(source, high, low):
        def one(i, carry):
            at = rows_of(i, block)
            high[at, :], low[at, :] = split(source[at, :])
            return carry

        lax.fori_loop(0, blocks, one, 0)

    loads[2].wait()
    halves(n_buf, nh, nl)
    sel_h[...] = dot(pick_t, nh[...]).astype(BF16)
    sel_l[...] = dot(pick_t, nl[...]).astype(BF16)
    nph[...] = dot(sel_h[...], perm_t[...]).astype(BF16)
    npl[...] = dot(sel_l[...], perm_t[...]).astype(BF16)
    base[...] = dot3((sel_h[...], sel_l[...]), field)
    loads[3].wait()
    halves(d_buf, dh, dl)

    def pick_d(i, carry):
        at = rows_of(i, block)
        deh[at, :] = dot(dh[at, :], pick).astype(BF16)
        del_[at, :] = dot(dl[at, :], pick).astype(BF16)
        return carry

    lax.fori_loop(0, blocks, pick_d, 0)
    outs = [
        pltpu.make_async_copy(src, dst, out_sem.at[i])
        for i, (src, dst) in enumerate(
            [(deh, deh_hbm), (del_, del_hbm), (sol, t1_hbm), (res, t2_hbm)]
        )
    ]
    outs[0].start()
    outs[1].start()

    def pick_pd(i, carry):
        at = rows_of(i, block)
        pdeh[at, :] = dot(perm[at, :], deh[...]).astype(BF16)
        pdel[at, :] = dot(perm[at, :], del_[...]).astype(BF16)
        return carry

    lax.fori_loop(0, blocks, pick_pd, 0)

    order = [
        (dz, d)
        for dz in sorted(range(nz), key=lambda dz: -min(dz, nz - dz))
        for d in range(ng)
        if (dz, d) != (0, 0)
    ]

    def spread(step, dz, d):
        return remote(
            psend.at[step, mate_at[d]],
            gath.at[step, me],
            a_ssem.at[step, dz, d],
            g_rsem.at[step, me],
            a,
            ((z + dz) % nz) * ng + mate_at[d],
        )

    def arrived(step, who):
        remote(
            psend.at[step, 0], gath.at[step, who], a_ssem.at[step, 0, 0], g_rsem.at[step, who],
            a, partner,
        ).wait_recv()

    def q_copy(step, d):
        return remote(
            qsend.at[step, mate_at[d]], cown.at[step, g], q_ssem.at[step, d], q_rsem.at[step, g],
            a, mates[d],
        )

    def first_copy(step, d):
        return remote(
            qsend.at[step, mate_at[d]], cprev.at[step, g], p_ssem.at[step, d], p_rsem.at[step, g],
            a + 1, mates[d],
        )

    def next_copy(step, q):
        return remote(
            csend.at[step, q], cprev.at[step, q], p_ssem.at[step, q], p_rsem.at[step, q],
            a + 1, me,
        )

    starts = jnp.logical_and(a == 0, a < nx - 1)
    passes = jnp.logical_and(a > 0, a < nx - 1)

    for step in range(STEPS):
        last = step + 1 == STEPS
        source = r_buf if step == 0 else res
        for k in (2, 3, 0, 1):
            pl.when(has[k])(functools.partial(face_wait, step, k))
        ghost = split(frecv[step])
        prim = base[...] - dot3((nph[...], npl[...]), ghost)
        for q in range(ng):
            psend[step, q] = pack(prim[:, q * part : (q + 1) * part])
        for dz, d in order:
            spread(step, dz, d).start()
        gath[step, me] = psend[step, g]

        def fill(i, carry, source=source, ghost=ghost):
            at = rows_of(i, block)
            back = perm_t[at, :]
            jump[at, :] = source[at, :] - dot(back, ghost[0]) - dot(back, ghost[1])
            return carry

        lax.fori_loop(0, blocks, fill, 0)
        jumps = split(jump[...])

        def multiply(i, carry, jumps=jumps):
            at = rows_of(i, block)
            upd[at, :] = dot3((nh[at, :], nl[at, :]), jumps)
            return carry

        lax.fori_loop(0, blocks, multiply, 0)
        works = split(upd[...])
        if step == 0:
            for dy in range(1, ny):
                coarse_arrived(((y + dy) % ny) * 2 + core)
                coarse_near(dy).start()

        def smooth(i, carry, works=works, step=step):
            at = rows_of(i, block)
            update = dot3((dh[at, :], dl[at, :]), works)
            if step == 0:
                sol[at, :] = update
            else:
                sol[at, :] += update
            res[at, :] = jump[at, :] - 0.5 * update
            return carry

        lax.fori_loop(0, blocks // 2, smooth, 0)
        if step == 0:
            for dy in range(ny):
                coarse_arrived(((y + dy) % ny) * 2 + 1 - core)
        coarse = split(c_all[...].reshape(ng * prims, c_all.shape[2]))
        for dz, d in order:
            arrived(step, ((z + dz) % nz) * ng + mate_at[d])
        values = jnp.concatenate([unpack(gath[step, b]) for b in range(ny_all)], axis=0)
        quarter = dot3(coarse, split(values))
        for q in range(ng):
            qsend[step, q] = pack(quarter[q * prims : (q + 1) * prims, :])

        @pl.when(starts)
        def _(step=step):
            for d in range(ng):
                first_copy(step, d).start()

        for d in range(1, ng):
            q_copy(step, d).start()
        cown[step, g] = qsend[step, g]
        lax.fori_loop(blocks // 2, blocks, smooth, 0)
        if last:
            outs[2].start()
            outs[3].start()
        else:
            rests = split(res[...])
            for k in range(4):
                pl.when(has[k])(functools.partial(take_face, step + 1, k, rests))
        for d in range(1, ng):
            remote(
                qsend.at[step, 0], cown.at[step, mate_at[d]], q_ssem.at[step, 0],
                q_rsem.at[step, mate_at[d]], a, partner,
            ).wait_recv()

        def joined(ref, step=step):
            return jnp.concatenate([unpack(ref[step, q]) for q in range(ng)], axis=1)

        @pl.when(a == 0)
        def _(step=step):
            chain_ref[...] = joined(cown)

        @pl.when(a > 0)
        def _(step=step):
            for q in range(ng):
                next_copy(step, q).wait_recv()
            chain_ref[...] = joined(cown) + rate * joined(cprev)

        @pl.when(passes)
        def _(step=step):
            for q in range(ng):
                csend[step, q] = pack(chain_ref[:, q * part : (q + 1) * part])
                next_copy(step, q).start()

        if not last:
            chain = split(chain_ref[...])

            def late_face(k, step=step, chain=chain):
                at = pl.ds(k * face, face)
                fsend[step + 1, at, :] -= 0.5 * dot3((pdeh[at, :], pdel[at, :]), chain)
                face_copy(step + 1, k).start()

            for k in range(4):
                pl.when(has[k])(functools.partial(late_face, k))

            def finish(i, carry, chain=chain):
                at = rows_of(i, block)
                more = dot3((deh[at, :], del_[at, :]), chain)
                sol[at, :] += more
                res[at, :] -= 0.5 * more
                return carry

            lax.fori_loop(0, blocks, finish, 0)
            base[...] = dot3((sel_h[...], sel_l[...]), split(res[...]))

    for out in outs:
        out.wait()
    coarse_near(0).wait_send()
    for dy in range(1, ny):
        coarse_far(dy).wait_send()
        coarse_near(dy).wait_send()
    for step in range(STEPS):
        for k in range(4):
            pl.when(has[k])(face_copy(step, k).wait_send)
        for dz, d in order:
            spread(step, dz, d).wait_send()
        for d in range(1, ng):
            q_copy(step, d).wait_send()

        @pl.when(starts)
        def _(step=step):
            for d in range(ng):
                first_copy(step, d).wait_send()

        @pl.when(passes)
        def _(step=step):
            for q in range(ng):
                next_copy(step, q).wait_send()


def closing(t1, t2, deh, del_, chain, sol, res):
    more = dot3((deh[...], del_[...]), split(chain[...]))
    sol[...] = t1[...] + more
    res[...] = t2[...] - 0.5 * more


def local(nx, ny_all, residual_in, neumann, dirichlet, coarse, decay, face_rows, primal):
    unknowns, width = residual_in.shape[2:]
    prims = primal.shape[2]
    order = coarse.shape[2]
    nz, ny = line_sizes(ny_all)
    ng = 2 * ny
    part = width // ng
    fold = max(1, 128 // part)
    piece = (prims // fold, fold * part)
    anywhere = pl.BlockSpec(memory_space=pl.ANY)
    inside = pl.BlockSpec(memory_space=pltpu.VMEM)
    square = (unknowns, unknowns)
    field = (unknowns, width)
    slim = (unknowns, prims)
    dma = pltpu.SemaphoreType.DMA
    whole = jax.ShapeDtypeStruct(field, F32)
    thin = jax.ShapeDtypeStruct(slim, BF16)
    pieces = pl.pallas_call(
        functools.partial(kernel, nx, ny_all),
        out_shape=(whole, whole, thin, thin, jax.ShapeDtypeStruct((prims, width), F32)),
        in_specs=[anywhere] * 4 + [inside] * 3,
        out_specs=(anywhere, anywhere, anywhere, anywhere, inside),
        scratch_shapes=[
            pltpu.VMEM(square, F32),
            pltpu.VMEM(square, F32),
        ]
        + [pltpu.VMEM(square, BF16)] * 6
        + [pltpu.VMEM(field, F32)] * 5
        + [
            pltpu.VMEM((STEPS,) + field, F32),
            pltpu.VMEM((STEPS,) + field, F32),
            pltpu.VMEM((ng, prims, order), F32),
            pltpu.VMEM((STEPS, ng) + piece, F32),
            pltpu.VMEM((STEPS, ny_all) + piece, F32),
            pltpu.VMEM((STEPS, ng) + piece, F32),
            pltpu.VMEM((STEPS, ng) + piece, F32),
            pltpu.VMEM((STEPS, ng) + piece, F32),
            pltpu.VMEM((STEPS, ng) + piece, F32),
        ]
        + [pltpu.VMEM((prims, unknowns), BF16)] * 4
        + [pltpu.VMEM(slim, BF16)] * 4
        + [
            pltpu.VMEM((prims, width), F32),
            dma((4,)),
            dma((4,)),
            dma((ny,)),
            dma((ny,)),
            dma((ng,)),
            dma((STEPS, 4)),
            dma((STEPS, 4)),
            dma((STEPS, nz, ng)),
            dma((STEPS, ny_all)),
            dma((STEPS, ng)),
            dma((STEPS, ng)),
            dma((STEPS, ng)),
            dma((STEPS, ng)),
        ],
        compiler_params=pltpu.CompilerParams(
            collective_id=0, has_side_effects=True, vmem_limit_bytes=60000 * 1024
        ),
    )(
        residual_in[0, 0],
        neumann[0, 0],
        dirichlet[0, 0],
        coarse[0],
        decay[0],
        face_rows[0],
        primal[0],
    )
    rows = unknowns // 2
    tall = pl.BlockSpec((rows, width), lambda i: (i, 0))
    thin_block = pl.BlockSpec((rows, prims), lambda i: (i, 0))
    fixed = pl.BlockSpec((prims, width), lambda i: (0, 0))
    sol, res = pl.pallas_call(
        closing,
        grid=(2,),
        out_shape=(whole, whole),
        in_specs=[tall, tall, thin_block, thin_block, fixed],
        out_specs=(tall, tall),
    )(*pieces)
    return (sol[None, None], res[None, None])


def solution(mesh):
    return jax.shard_map(
        functools.partial(local, mesh.shape["gx"], mesh.shape["gy"]),
        mesh=mesh,
        in_specs=(
            P("gx", "gy", None, None),
            P("gx", "gy", None, None),
            P("gx", "gy", None, None),
            P("gx", "gy", None),
            P("gx", "gy", None),
            P("gx", "gy", None),
            P("gx", "gy", None),
        ),
        out_specs=(P("gx", "gy", None, None), P("gx", "gy", None, None)),
        check_vma=False,
    )
```

profile of v0, /device:TPU:0, one launch (start us, length us, event | category | flops | bytes accessed | tf_op | source)
XLA Modules:
  0.0 53.9 jit_solution(8078768343416608903)
XLA Ops:
  0.6 50.0 %shard_map.86 = (f32[1024,256]{1,0:T(8,128)}, f32[1024,256]{1,0:T(8,128)}, bf16[1024,64]{1,0:T(8,128)(2,1)}, bf16[1024,64]{1,0:T(8,128)(2,1)}, f32[64,256]{1,0:T(8,128)}) custom-call(f32[1024,256]{1,0:T(8,128)} %bitcast.11, f32[1024,1024]{1,0:T(8,128)} %bitcast.9, f32[1024,1024]{1,0:T(8,128)} %bitcast.10, f32[64,1024]{1,0:T(8,128)} %bitcast.12, ...), custom_call_target="tpu_custom_call" | custom-call | tf_op jit(solution)/shard_map/pallas_call | solution.py:467
  50.7 3.3 %shard_map.87 = (f32[1024,256]{1,0:T(8,128)}, f32[1024,256]{1,0:T(8,128)}) custom-call(f32[1024,256]{1,0:T(8,128)} %get-tuple-element.9.t1, f32[1024,256]{1,0:T(8,128)} %get-tuple-element.10.t2, bf16[1024,64]{1,0:T(8,128)(2,1)} %get-tuple-element.11.deh, bf16[1024,64]{1,0:T(8,128)(2,1)} %get-tuple-element.12.del_, f32[64,256]{1,0:T(8,128)} %get-tuple-element.13.chain), custom_call_target="tpu_custom_call" | custom-call | tf_op jit(solution)/shard_map/pallas_call | solution.py:523
where the time goes:
time: 54.2 us; the launch traced here: 53.9 us
  Pallas kernels  53.3 us (98%)
  between operations  0.64 us (1%)
    pallas_call x1, Pallas kernels, local(): pl.pallas_call(functools.partial(kernel, nx, ny_all), out_shape=(whole, w...  50 us
    pallas_call x1, Pallas kernels, local(): pl.pallas_call(closing, grid=(2,), out_shape=(whole, whole), in_specs=[ta...  3.26 us

commit v1 on v0

v1 whole, which is shorter than its diff:
```python
import functools

import jax
import jax.numpy as jnp
from jax import lax
from jax.experimental import pallas as pl
from jax.experimental.pallas import tpu as pltpu
from jax.sharding import PartitionSpec as P

STEPS = 2
CUTS = (2, 3)
MESH = pl.DeviceIdType.MESH
F32 = jnp.float32
BF16 = jnp.bfloat16


def dot(a, b):
    return jnp.dot(a, b, preferred_element_type=F32)


def split(x):
    high = x.astype(BF16)
    return high, (x - high.astype(F32)).astype(BF16)


def dot3(a, b):
    return dot(a[0], b[0]) + dot(a[0], b[1]) + dot(a[1], b[0])


def stacked3(a, b):
    rows = a.shape[0] // 2
    first = dot(a, b[0])
    return first[:rows] + first[rows:] + dot(a[:rows], b[1])


def tall3(x):
    high, low = split(x)
    return jnp.concatenate([high, low, high], axis=0)


def when(cond, body):
    if cond is True:
        body()
    else:
        pl.when(cond)(body)


def line_sizes(count):
    chips = count // 2
    inner = 1
    while inner * inner * 4 <= chips:
        inner *= 2
    return chips // inner, inner


def x_slots(nx):
    return 1 if nx == 2 else 2


def kernel(
    nx, ny_all, r_hbm, n_hbm, d_hbm, c_hbm, decay_hbm, rows_hbm, prim_hbm,
    t1_ref, t2_ref, thin_ref, last_ref,
    n_buf, d_buf, nh, nl, dh, dl, perm, perm_t,
    r_buf, jump, upd, fsend, frecv, fix, c_all, cs, psend, gath, qsend, cown, cprev, csend,
    sel, npp, base, decay_v, rows_v, prim_v, esend, erecv, edges, chain_v, hsend, hrecv,
    load_sem, small_sem, cf_ssem, cp_ssem, c_rsem, f_ssem, f_rsem, a_ssem, g_rsem,
    q_ssem, q_rsem, p_ssem, p_rsem, e_ssem, e_rsem, h_ssem, h_rsem, line_sem,
):
    unknowns, width = r_buf.shape
    face = unknowns // 4
    prims = c_all.shape[1]
    nz, ny = line_sizes(ny_all)
    ng = 2 * ny
    part = width // ng
    fold = max(1, 128 // part)
    short = prims // fold
    block = 2 * face
    blocks = unknowns // block
    xs = x_slots(nx)
    slots = xs + 2

    a = lax.axis_index("gx")
    me = lax.axis_index("gy")
    plane = 2 * ny
    core = me % 2
    y = me // 2 % ny
    z = me // plane
    partner = me + 1 - 2 * core

    team = z // ny * ny + y
    g = z % ny * 2 + core

    def member(which, j):
        return ((which // ny * ny + j // 2) * ny + which % ny) * 2 + j % 2

    smalls = [
        pltpu.make_async_copy(src, dst, small_sem.at[i])
        for i, (src, dst) in enumerate(
            [(rows_hbm, rows_v), (prim_hbm, prim_v), (decay_hbm, decay_v)]
        )
    ]
    loads = [
        pltpu.make_async_copy(src, dst, load_sem.at[i])
        for i, (src, dst) in enumerate(
            [(r_hbm, r_buf), (c_hbm, c_all.at[g]), (n_hbm, n_buf), (d_hbm, d_buf)]
        )
    ]
    smalls[0].start()
    loads[0].start()
    smalls[1].start()
    smalls[2].start()

    barrier = pltpu.get_barrier_semaphore()

    def greet(gx, gy):
        pl.semaphore_signal(barrier, inc=1, device_id=(gx, gy), device_id_type=MESH)

    out_slot = xs + core
    in_slot = xs + 1 - core
    outward = me - 1 + 2 * core
    has_out = jnp.logical_and(outward >= 0, outward < ny_all)
    links = [(has_out, (a, outward), out_slot, in_slot)]
    if nx == 2:
        links.append((True, (1 - a, me), 0, 0))
    else:
        links.append((a > 0, (a - 1, me), 0, 1))
        links.append((a < nx - 1, (a + 1, me), 1, 0))
    links.append((True, (a, partner), in_slot, out_slot))
    mate_at = [(g + d) % ng for d in range(ng)]
    mates = [member(team, j) for j in mate_at]
    below, above = z > 0, z < nz - 1
    count = jnp.int32(ng - 1 + plane - 1)
    for has, where, _, _ in links[:-1]:
        when(has, functools.partial(greet, *where))
        count = count + (1 if has is True else has.astype(jnp.int32))
    for d in range(1, ng):
        greet(a, mates[d])
    for d in range(1, plane):
        greet(a, z * plane + (me + d) % plane)
    pl.when(below)(functools.partial(greet, a, me - plane))
    pl.when(above)(functools.partial(greet, a, me + plane))
    count = count + below.astype(jnp.int32) + above.astype(jnp.int32)
    if nx > 1:

        @pl.when(a < 2)
        def _():
            for d in range(1, ng):
                greet(1 - a, mates[d])

        count = count + (a < 2).astype(jnp.int32) * (ng - 1)

    def line_round(turn):
        def tell(low):
            pl.semaphore_signal(
                line_sem.at[turn, 1 if low else 0],
                inc=1,
                device_id=(a, me - plane if low else me + plane),
                device_id_type=MESH,
            )

        pl.when(below)(functools.partial(tell, True))
        pl.when(above)(functools.partial(tell, False))

    def line_wait(turn):
        pl.when(below)(lambda: pl.semaphore_wait(line_sem.at[turn, 0], 1))
        pl.when(above)(lambda: pl.semaphore_wait(line_sem.at[turn, 1], 1))

    turns = [0]

    def advance():
        turn = turns[0]
        if turn < nz - 1:
            line_wait(turn)
            if turn + 1 < nz - 1:
                line_round(turn + 1)
            turns[0] = turn + 1

    def pack(x, pieces=fold):
        size = x.shape[0] // pieces
        return jnp.concatenate([x[j * size : (j + 1) * size] for j in range(pieces)], axis=1)

    def unpack(x, columns=part):
        return jnp.concatenate(
            [x[:, j * columns : (j + 1) * columns] for j in range(x.shape[1] // columns)], axis=0
        )

    def rows_of(i, size):
        if isinstance(i, int):
            return pl.ds(i * size, size)
        return pl.ds(pl.multiple_of(i * size, size), size)

    def remote(src, dst, send, recv, gx, gy):
        return pltpu.make_async_remote_copy(
            src_ref=src, dst_ref=dst, send_sem=send, recv_sem=recv,
            device_id=(gx, gy), device_id_type=MESH,
        )

    def face_copy(step, link):
        _, where, here, there = link
        return remote(
            fsend.at[step, rows_of(here, face), :],
            frecv.at[step, rows_of(there, face), :],
            f_ssem.at[step, here],
            f_rsem.at[step, there],
            *where,
        )

    def face_part(step, link, first, stop):
        _, where, here, there = link
        size = face // 4

        def part_of(slot):
            start = slot * face + first * size
            if not isinstance(slot, int):
                start = pl.multiple_of(start, size)
            return pl.ds(start, (stop - first) * size)

        return remote(
            fsend.at[step, part_of(here), :],
            frecv.at[step, part_of(there), :],
            f_ssem.at[step, here],
            f_rsem.at[step, there],
            *where,
        )

    def send_part(step, first, stop):
        for link in links[:-1]:
            when(link[0], face_part(step, link, first, stop).start)

    def edge_copy(link):
        _, where, here, there = link
        return remote(
            esend.at[here], erecv.at[there], e_ssem.at[here], e_rsem.at[there], *where
        )

    def chain_copy(step, link):
        _, where, here, there = link
        return remote(
            hsend.at[step], hrecv.at[step, there], h_ssem.at[step, here], h_rsem.at[step, there],
            *where,
        )

    def arrives(copy, link):
        has, where, here, _ = link
        when(has, copy((has, where, here, here)).wait_recv)

    lanes = 128

    def face_lines(slot):
        if nx == 2:
            number = 1 - a if isinstance(slot, int) and slot == 0 else slot + 1
        else:
            number = slot
        return rows_v[:, rows_of(number, face)].astype(F32)

    def build_face(slot):
        column = jnp.transpose(jnp.broadcast_to(face_lines(slot), (lanes, face)))
        for t in range(unknowns // lanes):
            cols = lax.broadcasted_iota(jnp.int32, (face, lanes), 1) + t * lanes
            perm[rows_of(slot, face), t * lanes : (t + 1) * lanes] = jnp.where(
                column == cols.astype(F32), 1.0, 0.0
            ).astype(BF16)

    def take_faces(step, field):
        fsend[step] = dot(perm[...], field[0]) + dot(perm[...], field[1])

    smalls[0].wait()
    for slot in range(slots):
        build_face(slot)
    loads[0].wait()
    for load in loads[1:]:
        load.start()
    field = split(r_buf[...])
    take_faces(0, field)
    pl.semaphore_wait(barrier, count)
    for link in links:
        when(link[0], face_copy(0, link).start)
    if nz > 1:
        line_round(0)

    along = [(z + dy) % ny for dy in range(ny)]

    def coarse_far(dy):
        return remote(
            c_all.at[g], c_all.at[g], cf_ssem.at[dy], c_rsem.at[g],
            a, member(team, along[dy] * 2 + core),
        )

    def coarse_near(dy):
        which = along[dy] * 2 + core
        return remote(
            c_all.at[which], c_all.at[which], cp_ssem.at[dy], c_rsem.at[which], a, partner
        )

    def coarse_arrived(which):
        remote(
            c_all.at[which], c_all.at[which], cp_ssem.at[0], c_rsem.at[which], a, partner
        ).wait_recv()

    loads[1].wait()
    coarse_near(0).start()
    for dy in range(1, ny):
        coarse_far(dy).start()

    for link in links[:-1]:
        if link[0] is not True:

            @pl.when(jnp.logical_not(link[0]))
            def _(link=link):
                here = link[2]
                for step in range(STEPS):
                    frecv[step, rows_of(here, face), :] = jnp.zeros((face, width), F32)
                erecv[here] = jnp.zeros(erecv.shape[1:], F32)
                for step in range(STEPS - 1):
                    hrecv[step, here] = jnp.zeros((prims, width), F32)

    lines = jnp.concatenate([face_lines(slot) for slot in range(slots)], axis=1)

    def build_t(i, carry):
        at = rows_of(i, block)
        here = lax.broadcasted_iota(jnp.int32, (block, slots * face), 0) + i * block
        perm_t[at, :] = jnp.where(here.astype(F32) == lines, 1.0, 0.0).astype(BF16)
        return carry

    lax.fori_loop(0, blocks, build_t, 0)

    smalls[1].wait()
    smalls[2].wait()
    eye = lax.broadcasted_iota(jnp.int32, (prims, prims), 0) == lax.broadcasted_iota(
        jnp.int32, (prims, prims), 1
    )
    prim_row = prim_v[...].astype(F32)
    prim_col = jnp.sum(jnp.where(eye, prim_row, 0.0), axis=1, keepdims=True)
    rate = jnp.sum(jnp.where(eye, decay_v[...], 0.0), axis=1, keepdims=True)
    pick_t = jnp.where(
        prim_col == lax.broadcasted_iota(jnp.int32, (prims, unknowns), 1).astype(F32), 1.0, 0.0
    ).astype(BF16)
    thrice = jnp.concatenate([prim_row] * 3, axis=1)
    tops = lax.broadcasted_iota(jnp.int32, (unknowns, 3 * prims), 0).astype(F32) == thrice
    high_side = lax.broadcasted_iota(jnp.int32, (unknowns, 3 * prims), 1) < 2 * prims
    pick_h = jnp.where(jnp.logical_and(tops, high_side), 1.0, 0.0).astype(BF16)
    pick_l = jnp.where(
        jnp.logical_and(tops, jnp.logical_not(high_side)), 1.0, 0.0
    ).astype(BF16)

    loads[2].wait()

    def halve(i, carry):
        at = rows_of(i, block)
        nh[at, :], nl[at, :] = split(n_buf[at, :])
        return carry

    lax.fori_loop(0, blocks, halve, 0)
    advance()
    sel[0:prims, :] = dot(pick_t, nh[...]).astype(BF16)
    sel[prims : 2 * prims, :] = dot(pick_t, nl[...]).astype(BF16)
    advance()
    npp[...] = dot(sel[...], perm_t[...]).astype(BF16)
    base[...] = stacked3(sel[...], field)
    advance()
    loads[3].wait()

    def halve_pick(i, carry):
        at = rows_of(i, block)
        high, low = split(d_buf[at, :])
        dh[at, :] = high
        dl[at, :] = low
        thin_ref[at, :] = (dot(high, pick_h) + dot(low, pick_l)).astype(BF16)
        return carry

    lax.fori_loop(0, blocks, halve_pick, 0)
    for _ in range(nz):
        advance()
    lifted = dot(perm[...], thin_ref[...])
    lifted = lifted[:, :prims] + lifted[:, 2 * prims :]
    for slot in range(slots):
        esend[slot] = pack(lifted[slot * face : (slot + 1) * face], 128 // prims)
    for link in links:
        when(link[0], edge_copy(link).start)

    order = [
        (dz, d)
        for dz in sorted(range(nz), key=lambda dz: -min(dz, nz - dz))
        for d in range(ng)
        if (dz, d) != (0, 0)
    ]

    def spread(step, dz, d):
        return remote(
            psend.at[step, mate_at[d]],
            gath.at[step, me],
            a_ssem.at[step, dz, d],
            g_rsem.at[step, me],
            a,
            member((team + dz) % nz, mate_at[d]),
        )

    def arrived(step, who):
        remote(
            psend.at[step, 0], gath.at[step, who], a_ssem.at[step, 0, 0], g_rsem.at[step, who],
            a, partner,
        ).wait_recv()

    def q_copy(step, d):
        return remote(
            qsend.at[step, mate_at[d]], cown.at[step, g], q_ssem.at[step, d], q_rsem.at[step, g],
            a, mates[d],
        )

    def first_copy(step, d):
        return remote(
            qsend.at[step, mate_at[d]], cprev.at[step, g], p_ssem.at[step, d], p_rsem.at[step, g],
            a + 1, mates[d],
        )

    def next_copy(step, q):
        return remote(
            csend.at[step, q], cprev.at[step, q], p_ssem.at[step, q], p_rsem.at[step, q],
            a + 1, me,
        )

    starts = jnp.logical_and(a == 0, a < nx - 1)
    passes = jnp.logical_and(a > 0, a < nx - 1)

    for step in range(STEPS):
        last = step + 1 == STEPS
        source = r_buf if step == 0 else t2_ref
        for link in links:
            arrives(functools.partial(face_copy, step), link)
        if step == 0:
            ghost = split(frecv[step])
        else:
            ghost = split(frecv[step] - fix[...])
        prim = base[...] - stacked3(npp[...], ghost)
        for q in range(ng):
            psend[step, q] = pack(prim[:, q * part : (q + 1) * part])
        for dz, d in order:
            spread(step, dz, d).start()
        gath[step, me] = psend[step, g]

        def fill(i, carry, source=source, ghost=ghost):
            at = rows_of(i, block)
            back = perm_t[at, :]
            jump[at, :] = source[at, :] - dot(back, ghost[0]) - dot(back, ghost[1])
            return carry

        lax.fori_loop(0, blocks, fill, 0)
        jumps = split(jump[...])

        def multiply(i, carry, jumps=jumps):
            at = rows_of(i, block)
            upd[at, :] = dot3((nh[at, :], nl[at, :]), jumps)
            return carry

        lax.fori_loop(0, blocks, multiply, 0)
        if step == 0:
            for dy in range(1, ny):
                coarse_arrived(along[dy] * 2 + core)
                coarse_near(dy).start()
        works = split(upd[...])

        def smooth(i, carry, works=works, step=step):
            at = rows_of(i, block)
            update = dot3((dh[at, :], dl[at, :]), works)
            if step == 0:
                t1_ref[at, :] = update
            else:
                t1_ref[at, :] += update
            t2_ref[at, :] = jump[at, :] - 0.5 * update
            return carry

        lax.fori_loop(0, blocks, smooth, 0)
        if not last:
            take_faces(step + 1, split(t2_ref[...]))
            send_part(step + 1, 0, CUTS[0])
            face_copy(step + 1, links[-1]).start()
        if step == 0:
            for dy in range(ny):
                coarse_arrived(along[dy] * 2 + 1 - core)
            size = ng * prims
            cs[0:size, :], cs[size : 2 * size, :] = split(
                c_all[...].reshape(size, c_all.shape[2])
            )
        for dz, d in order:
            arrived(step, member((team + dz) % nz, mate_at[d]))
        values = jnp.concatenate([unpack(gath[step, b]) for b in range(ny_all)], axis=0)
        quarter = stacked3(cs[...], split(values))
        for q in range(ng):
            qsend[step, q] = pack(quarter[q * prims : (q + 1) * prims, :])

        @pl.when(starts)
        def _(step=step):
            for d in range(ng):
                first_copy(step, d).start()

        for d in range(1, ng):
            q_copy(step, d).start()
        if not last:
            send_part(step + 1, CUTS[0], CUTS[1])
        cown[step, g] = qsend[step, g]
        if step == 0:
            for link in links:
                arrives(edge_copy, link)
            for slot in range(slots):
                high, low = split(unpack(erecv[slot], prims))
                edges[slot * face : (slot + 1) * face, :] = jnp.concatenate(
                    [high, high, low], axis=1
                )
        for d in range(1, ng):
            remote(
                qsend.at[step, 0], cown.at[step, mate_at[d]], q_ssem.at[step, 0],
                q_rsem.at[step, mate_at[d]], a, partner,
            ).wait_recv()

        def joined(ref, step=step):
            return jnp.concatenate([unpack(ref[step, q]) for q in range(ng)], axis=1)

        @pl.when(a == 0)
        def _(step=step):
            chain_v[...] = joined(cown)

        @pl.when(a > 0)
        def _(step=step):
            for q in range(ng):
                next_copy(step, q).wait_recv()
            chain_v[...] = joined(cown) + rate * joined(cprev)

        @pl.when(passes)
        def _(step=step):
            for q in range(ng):
                csend[step, q] = pack(chain_v[:, q * part : (q + 1) * part])
                next_copy(step, q).start()

        if last:
            last_ref[...] = chain_v[...]
        else:
            hsend[step] = chain_v[...]
            for link in links:
                when(link[0], chain_copy(step, link).start)
            send_part(step + 1, CUTS[1], 4)
            chain = tall3(chain_v[...])

            def finish(i, carry, chain=chain):
                at = rows_of(i, block)
                more = dot(thin_ref[at, :], chain)
                t1_ref[at, :] += more
                t2_ref[at, :] -= 0.5 * more
                return carry

            lax.fori_loop(0, blocks, finish, 0)
            base[...] = stacked3(sel[...], split(t2_ref[...]))
            for link in links:
                arrives(functools.partial(chain_copy, step), link)
            for slot in range(slots):
                at = slice(slot * face, (slot + 1) * face)
                fix[at, :] = 0.5 * dot(edges[at, :], tall3(hrecv[step, slot]))

    coarse_near(0).wait_send()
    for dy in range(1, ny):
        coarse_far(dy).wait_send()
        coarse_near(dy).wait_send()
    for link in links:
        when(link[0], edge_copy(link).wait_send)
    for step in range(STEPS):
        for link in links:
            when(link[0], face_copy(step, link).wait_send)
            if step + 1 < STEPS:
                when(link[0], chain_copy(step, link).wait_send)
        for dz, d in order:
            spread(step, dz, d).wait_send()
        for d in range(1, ng):
            q_copy(step, d).wait_send()

        @pl.when(starts)
        def _(step=step):
            for d in range(ng):
                first_copy(step, d).wait_send()

        @pl.when(passes)
        def _(step=step):
            for q in range(ng):
                next_copy(step, q).wait_send()


def closing(t1, t2, thin, chain, sol, res):
    rows = sol.shape[0]
    at = pl.ds(pl.multiple_of(pl.program_id(0) * rows, rows), rows)
    more = dot(thin[at, :], tall3(chain[...]))
    sol[...] = t1[at, :] + more
    res[...] = t2[at, :] - 0.5 * more


def local(nx, ny_all, residual_in, neumann, dirichlet, coarse, decay, face_rows, primal):
    unknowns, width = residual_in.shape[2:]
    prims = primal.shape[2]
    order = coarse.shape[2]
    nz, ny = line_sizes(ny_all)
    ng = 2 * ny
    part = width // ng
    fold = max(1, 128 // part)
    piece = (prims // fold, fold * part)
    face = unknowns // 4
    slots = x_slots(nx) + 2
    anywhere = pl.BlockSpec(memory_space=pl.ANY)
    inside = pl.BlockSpec(memory_space=pltpu.VMEM)
    square = (unknowns, unknowns)
    field = (unknowns, width)
    ghosts = (slots * face, width)
    edge = (slots, face * prims // 128, 128)
    dma = pltpu.SemaphoreType.DMA
    whole = jax.ShapeDtypeStruct(field, F32)
    outs = [(field, F32), (field, F32), ((unknowns, 3 * prims), BF16), ((prims, width), F32)]
    pieces = pl.pallas_call(
        functools.partial(kernel, nx, ny_all),
        out_shape=tuple(pltpu.VMEM(shape, kind) for shape, kind in outs),
        in_specs=[anywhere] * 7,
        out_specs=(inside,) * 4,
        scratch_shapes=[
            pltpu.VMEM(square, F32),
            pltpu.VMEM(square, F32),
        ]
        + [pltpu.VMEM(square, BF16)] * 4
        + [
            pltpu.VMEM((slots * face, unknowns), BF16),
            pltpu.VMEM((unknowns, slots * face), BF16),
        ]
        + [pltpu.VMEM(field, F32)] * 3
        + [
            pltpu.VMEM((STEPS,) + ghosts, F32),
            pltpu.VMEM((STEPS,) + ghosts, F32),
            pltpu.VMEM(ghosts, F32),
            pltpu.VMEM((ng, prims, order), F32),
            pltpu.VMEM((2 * ng * prims, order), BF16),
            pltpu.VMEM((STEPS, ng) + piece, F32),
            pltpu.VMEM((STEPS, ny_all) + piece, F32),
            pltpu.VMEM((STEPS, ng) + piece, F32),
            pltpu.VMEM((STEPS, ng) + piece, F32),
            pltpu.VMEM((STEPS, ng) + piece, F32),
            pltpu.VMEM((STEPS, ng) + piece, F32),
            pltpu.VMEM((2 * prims, unknowns), BF16),
            pltpu.VMEM((2 * prims, slots * face), BF16),
            pltpu.VMEM((prims, width), F32),
            pltpu.VMEM((1, prims), F32),
            pltpu.VMEM((1, unknowns), jnp.int32),
            pltpu.VMEM((1, prims), jnp.int32),
            pltpu.VMEM(edge, F32),
            pltpu.VMEM(edge, F32),
            pltpu.VMEM((slots * face, 3 * prims), BF16),
            pltpu.VMEM((prims, width), F32),
            pltpu.VMEM((STEPS - 1, prims, width), F32),
            pltpu.VMEM((STEPS - 1, slots, prims, width), F32),
            dma((4,)),
            dma((3,)),
            dma((ny,)),
            dma((ny,)),
            dma((ng,)),
            dma((STEPS, slots)),
            dma((STEPS, slots)),
            dma((STEPS, nz, ng)),
            dma((STEPS, ny_all)),
            dma((STEPS, ng)),
            dma((STEPS, ng)),
            dma((STEPS, ng)),
            dma((STEPS, ng)),
            dma((slots,)),
            dma((slots,)),
            dma((STEPS - 1, slots)),
            dma((STEPS - 1, slots)),
            pltpu.SemaphoreType.REGULAR((max(1, nz - 1), 2)),
        ],
        compiler_params=pltpu.CompilerParams(
            collective_id=0, has_side_effects=True, vmem_limit_bytes=62720 * 1024
        ),
    )(
        residual_in[0, 0],
        neumann[0, 0],
        dirichlet[0, 0],
        coarse[0],
        decay[0],
        face_rows[0],
        primal[0],
    )
    rows = unknowns // 4
    tall = pl.BlockSpec((rows, width), lambda i: (i, 0))
    sol, res = pl.pallas_call(
        closing,
        grid=(unknowns // rows,),
        out_shape=(whole, whole),
        in_specs=[inside] * 4,
        out_specs=(tall, tall),
        compiler_params=pltpu.CompilerParams(vmem_limit_bytes=16000 * 1024),
    )(*pieces)
    return (sol[None, None], res[None, None])


def solution(mesh):
    return jax.shard_map(
        functools.partial(local, mesh.shape["gx"], mesh.shape["gy"]),
        mesh=mesh,
        in_specs=(
            P("gx", "gy", None, None),
            P("gx", "gy", None, None),
            P("gx", "gy", None, None),
            P("gx", "gy", None),
            P("gx", "gy", None),
            P("gx", "gy", None),
            P("gx", "gy", None),
        ),
        out_specs=(P("gx", "gy", None, None), P("gx", "gy", None, None)),
        check_vma=False,
    )
```

time: 54.2 us -> 49 us (0.904)
  Pallas kernels: 53.3 us -> 48.2 us
    pallas_call x2, Pallas kernels: 53.3 us -> 48.2 us  [the longest x1 46 us: local(): pl.pallas_call(functools.partial(kernel, nx, ny_all), out_shape=tuple((pl...]
where the time goes in v1:
time: 49 us; the launch traced here: 48.8 us
  Pallas kernels  48.2 us (98%)
  between operations  0.64 us (1%)
    pallas_call x1, Pallas kernels, local(): pl.pallas_call(functools.partial(kernel, nx, ny_all), out_shape=tuple((pl...  46 us
    pallas_call x1, Pallas kernels, local(): pl.pallas_call(closing, grid=(unknowns // rows,), out_shape=(whole, whole...  2.16 us

profile of v1, /device:TPU:0, one launch (start us, length us, event | category | flops | bytes accessed | tf_op | source)
XLA Modules:
  0.0 48.8 jit_solution(145007692839109215)
XLA Ops:
  0.6 46.0 %shard_map.86 = (f32[1024,256]{1,0:T(8,128)S(1)}, f32[1024,256]{1,0:T(8,128)S(1)}, bf16[1024,192]{1,0:T(8,128)(2,1)S(1)}, f32[64,256]{1,0:T(8,128)S(1)}) custom-call(f32[1024,256]{1,0:T(8,128)} %bitcast.11, f32[1024,1024]{1,0:T(8,128)} %bitcast.9, f32[1024,1024]{1,0:T(8,128)} %bitcast.10, f32[64,1024]{1,0:T(8,128)} %bitcast.12, f32[1,64]{1,0:T(1,128)} %bitcast.14, ...), custom_call_target="tpu_custom_call" | custom-call | tf_op jit(solution)/shard_map/pallas_call | solution.py:613
  46.6 2.2 %shard_map.87 = (f32[1024,256]{1,0:T(8,128)}, f32[1024,256]{1,0:T(8,128)}) custom-call(f32[1024,256]{1,0:T(8,128)S(1)} %get-tuple-element.8.t1, f32[1024,256]{1,0:T(8,128)S(1)} %get-tuple-element.9.t2, bf16[1024,192]{1,0:T(8,128)(2,1)S(1)} %get-tuple-element.10.thin, f32[64,256]{1,0:T(8,128)S(1)} %get-tuple-element.11.chain), custom_call_target="tpu_custom_call" | custom-call | tf_op jit(solution)/shard_map/pallas_call | solution.py:685

commit v2 on v1

--- a/solution.py
+++ b/solution.py
@@ -8,7 +8,9 @@
 from jax.sharding import PartitionSpec as P
 
 STEPS = 2
-CUTS = (2, 3)
+CUTS = (0, 2, 4, 4)
+UP_CUTS = (0, 1, 4, 4)
+DOWN_CUTS = (0, 4, 4, 4)
 MESH = pl.DeviceIdType.MESH
 F32 = jnp.float32
 BF16 = jnp.bfloat16
@@ -41,8 +43,20 @@
 def when(cond, body):
     if cond is True:
         body()
-    else:
+    elif cond is not False:
         pl.when(cond)(body)
+
+
+def both(p, q):
+    if p is True or q is False:
+        return q
+    if q is True or p is False:
+        return p
+    return jnp.logical_and(p, q)
+
+
+def negate(p):
+    return not p if isinstance(p, bool) else jnp.logical_not(p)
 
 
 def line_sizes(count):
@@ -61,7 +75,7 @@
     nx, ny_all, r_hbm, n_hbm, d_hbm, c_hbm, decay_hbm, rows_hbm, prim_hbm,
     t1_ref, t2_ref, thin_ref, last_ref,
     n_buf, d_buf, nh, nl, dh, dl, perm, perm_t,
-    r_buf, jump, upd, fsend, frecv, fix, c_all, cs, psend, gath, qsend, cown, cprev, csend,
+    r_buf, jump, high_v, low_v, high_w, low_w, fsend, frecv, fix, c_all, cs, psend, gath, qsend, cown, cprev, csend,
     sel, npp, base, decay_v, rows_v, prim_v, esend, erecv, edges, chain_v, hsend, hrecv,
     load_sem, small_sem, cf_ssem, cp_ssem, c_rsem, f_ssem, f_rsem, a_ssem, g_rsem,
     q_ssem, q_rsem, p_ssem, p_rsem, e_ssem, e_rsem, h_ssem, h_rsem, line_sem,
@@ -119,18 +133,18 @@
     in_slot = xs + 1 - core
     outward = me - 1 + 2 * core
     has_out = jnp.logical_and(outward >= 0, outward < ny_all)
-    links = [(has_out, (a, outward), out_slot, in_slot)]
+    links = [(has_out, (a, outward), out_slot, in_slot, None)]
     if nx == 2:
-        links.append((True, (1 - a, me), 0, 0))
+        links.append((True, (1 - a, me), 0, 0, a == 0))
     else:
-        links.append((a > 0, (a - 1, me), 0, 1))
-        links.append((a < nx - 1, (a + 1, me), 1, 0))
-    links.append((True, (a, partner), in_slot, out_slot))
+        links.append((a > 0, (a - 1, me), 0, 1, False))
+        links.append((a < nx - 1, (a + 1, me), 1, 0, True))
+    links.append((True, (a, partner), in_slot, out_slot, None))
     mate_at = [(g + d) % ng for d in range(ng)]
     mates = [member(team, j) for j in mate_at]
     below, above = z > 0, z < nz - 1
     count = jnp.int32(ng - 1 + plane - 1)
-    for has, where, _, _ in links[:-1]:
+    for has, where, _, _, _ in links[:-1]:
         when(has, functools.partial(greet, *where))
         count = count + (1 if has is True else has.astype(jnp.int32))
     for d in range(1, ng):
@@ -196,7 +210,7 @@
         )
 
     def face_copy(step, link):
-        _, where, here, there = link
+        _, where, here, there, _ = link
         return remote(
             fsend.at[step, rows_of(here, face), :],
             frecv.at[step, rows_of(there, face), :],
@@ -206,7 +220,7 @@
         )
 
     def face_part(step, link, first, stop):
-        _, where, here, there = link
+        _, where, here, there, _ = link
         size = face // 4
 
         def part_of(slot):
@@ -223,26 +237,37 @@
             *where,
         )
 
-    def send_part(step, first, stop):
-        for link in links[:-1]:
-            when(link[0], face_part(step, link, first, stop).start)
+    def send_part(step, stage, some):
+        for link in some:
+            for up, cuts in ((None, CUTS), (True, UP_CUTS), (False, DOWN_CUTS)):
+                first, stop = cuts[stage], cuts[stage + 1]
+                if first == stop or (up is None) != (link[4] is None):
+                    continue
+                side = True if up is None else link[4] if up else negate(link[4])
+                when(both(link[0], side), face_part(step, link, first, stop).start)
 
     def edge_copy(link):
-        _, where, here, there = link
+        _, where, here, there, _ = link
         return remote(
             esend.at[here], erecv.at[there], e_ssem.at[here], e_rsem.at[there], *where
         )
 
     def chain_copy(step, link):
-        _, where, here, there = link
+        _, where, here, there, _ = link
         return remote(
             hsend.at[step], hrecv.at[step, there], h_ssem.at[step, here], h_rsem.at[step, there],
             *where,
         )
 
-    def arrives(copy, link):
-        has, where, here, _ = link
-        when(has, copy((has, where, here, here)).wait_recv)
+    def arrives(copy, link, cond=True):
+        has, where, here, _, up = link
+        when(both(has, cond), copy((has, where, here, here, up)).wait_recv)
+
+    def comes_down(link):
+        return True if link[4] is None else link[4]
+
+    def goes_down(link):
+        return True if link[4] is None else negate(link[4])
 
     lanes = 128
 
@@ -261,8 +286,11 @@
                 column == cols.astype(F32), 1.0, 0.0
             ).astype(BF16)
 
-    def take_faces(step, field):
-        fsend[step] = dot(perm[...], field[0]) + dot(perm[...], field[1])
+    def take_faces(step, field, some):
+        for slot in some:
+            at = slice(slot * face, (slot + 1) * face)
+            picks = perm[at, :]
+            fsend[step, at, :] = dot(picks, field[0]) + dot(picks, field[1])
 
     smalls[0].wait()
     for slot in range(slots):
@@ -271,9 +299,11 @@
     for load in loads[1:]:
         load.start()
     field = split(r_buf[...])
-    take_faces(0, field)
+    take_faces(0, field, range(xs, slots))
     pl.semaphore_wait(barrier, count)
-    for link in links:
+    when(links[0][0], face_copy(0, links[0]).start)
+    take_faces(0, field, range(xs))
+    for link in links[1:]:
         when(link[0], face_copy(0, link).start)
     if nz > 1:
         line_round(0)
@@ -342,7 +372,6 @@
     pick_l = jnp.where(
         jnp.logical_and(tops, jnp.logical_not(high_side)), 1.0, 0.0
     ).astype(BF16)
-
     loads[2].wait()
 
     def halve(i, carry):
@@ -441,15 +470,17 @@
         def fill(i, carry, source=source, ghost=ghost):
             at = rows_of(i, block)
             back = perm_t[at, :]
-            jump[at, :] = source[at, :] - dot(back, ghost[0]) - dot(back, ghost[1])
+            value = source[at, :] - dot(back, ghost[0]) - dot(back, ghost[1])
+            jump[at, :] = value
+            high_v[at, :], low_v[at, :] = split(value)
             return carry
 
         lax.fori_loop(0, blocks, fill, 0)
-        jumps = split(jump[...])
-
-        def multiply(i, carry, jumps=jumps):
+
+        def multiply(i, carry):
             at = rows_of(i, block)
-            upd[at, :] = dot3((nh[at, :], nl[at, :]), jumps)
+            work = dot3((nh[at, :], nl[at, :]), (high_v[...], low_v[...]))
+            high_w[at, :], low_w[at, :] = split(work)
             return carry
 
         lax.fori_loop(0, blocks, multiply, 0)
@@ -457,22 +488,27 @@
             for dy in range(1, ny):
                 coarse_arrived(along[dy] * 2 + core)
                 coarse_near(dy).start()
-        works = split(upd[...])
-
-        def smooth(i, carry, works=works, step=step):
+
+        def smooth(i, carry, step=step, last=last):
             at = rows_of(i, block)
-            update = dot3((dh[at, :], dl[at, :]), works)
+            update = dot3((dh[at, :], dl[at, :]), (high_w[...], low_w[...]))
             if step == 0:
                 t1_ref[at, :] = update
             else:
                 t1_ref[at, :] += update
-            t2_ref[at, :] = jump[at, :] - 0.5 * update
+            rest = jump[at, :] - 0.5 * update
+            t2_ref[at, :] = rest
+            if not last:
+                high_v[at, :], low_v[at, :] = split(rest)
             return carry
 
         lax.fori_loop(0, blocks, smooth, 0)
         if not last:
-            take_faces(step + 1, split(t2_ref[...]))
-            send_part(step + 1, 0, CUTS[0])
+            rests = (high_v[...], low_v[...])
+            take_faces(step + 1, rests, range(xs, slots))
+            send_part(step + 1, 0, links[:1])
+            take_faces(step + 1, rests, range(xs))
+            send_part(step + 1, 0, links[1:-1])
             face_copy(step + 1, links[-1]).start()
         if step == 0:
             for dy in range(ny):
@@ -496,16 +532,8 @@
         for d in range(1, ng):
             q_copy(step, d).start()
         if not last:
-            send_part(step + 1, CUTS[0], CUTS[1])
+            send_part(step + 1, 1, links[:-1])
         cown[step, g] = qsend[step, g]
-        if step == 0:
-            for link in links:
-                arrives(edge_copy, link)
-            for slot in range(slots):
-                high, low = split(unpack(erecv[slot], prims))
-                edges[slot * face : (slot + 1) * face, :] = jnp.concatenate(
-                    [high, high, low], axis=1
-                )
         for d in range(1, ng):
             remote(
                 qsend.at[step, 0], cown.at[step, mate_at[d]], q_ssem.at[step, 0],
@@ -536,8 +564,14 @@
         else:
             hsend[step] = chain_v[...]
             for link in links:
-                when(link[0], chain_copy(step, link).start)
-            send_part(step + 1, CUTS[1], 4)
+                when(both(link[0], goes_down(link)), chain_copy(step, link).start)
+            send_part(step + 1, 2, links[:-1])
+            if nx > 1:
+
+                @pl.when(a > 0)
+                def _(step=step):
+                    hrecv[step, 0] = joined(cprev)
+
             chain = tall3(chain_v[...])
 
             def finish(i, carry, chain=chain):
@@ -549,8 +583,16 @@
 
             lax.fori_loop(0, blocks, finish, 0)
             base[...] = stacked3(sel[...], split(t2_ref[...]))
+            if step == 0:
+                for link in links:
+                    arrives(edge_copy, link)
+                for slot in range(slots):
+                    high, low = split(unpack(erecv[slot], prims))
+                    edges[slot * face : (slot + 1) * face, :] = jnp.concatenate(
+                        [high, high, low], axis=1
+                    )
             for link in links:
-                arrives(functools.partial(chain_copy, step), link)
+                arrives(functools.partial(chain_copy, step), link, comes_down(link))
             for slot in range(slots):
                 at = slice(slot * face, (slot + 1) * face)
                 fix[at, :] = 0.5 * dot(edges[at, :], tall3(hrecv[step, slot]))
@@ -565,7 +607,7 @@
         for link in links:
             when(link[0], face_copy(step, link).wait_send)
             if step + 1 < STEPS:
-                when(link[0], chain_copy(step, link).wait_send)
+                when(both(link[0], goes_down(link)), chain_copy(step, link).wait_send)
         for dz, d in order:
             spread(step, dz, d).wait_send()
         for d in range(1, ng):
@@ -624,7 +666,8 @@
             pltpu.VMEM((slots * face, unknowns), BF16),
             pltpu.VMEM((unknowns, slots * face), BF16),
         ]
-        + [pltpu.VMEM(field, F32)] * 3
+        + [pltpu.VMEM(field, F32)] * 2
+        + [pltpu.VMEM(field, BF16)] * 4
         + [
             pltpu.VMEM((STEPS,) + ghosts, F32),
             pltpu.VMEM((STEPS,) + ghosts, F32),

time: 49 us -> 46.6 us (0.951)
  Pallas kernels: 48.2 us -> 45.8 us
    pallas_call x1, Pallas kernels: 46 us -> 43.6 us  [local(): pl.pallas_call(functools.partial(kernel, nx, ny_all), out_shape=tuple((pl...]
where the time goes in v2:
time: 46.6 us; the launch traced here: 46.4 us
  Pallas kernels  45.8 us (98%)
  between operations  0.64 us (1%)
    pallas_call x1, Pallas kernels, local(): pl.pallas_call(functools.partial(kernel, nx, ny_all), out_shape=tuple((pl...  43.6 us
    pallas_call x1, Pallas kernels, local(): pl.pallas_call(closing, grid=(unknowns // rows,), out_shape=(whole, whole...  2.17 us

profile of v2, /device:TPU:0, one launch (start us, length us, event | category | flops | bytes accessed | tf_op | source)
XLA Modules:
  0.0 46.4 jit_solution(5267410079569333873)
XLA Ops:
  0.6 43.6 %shard_map.86 = (f32[1024,256]{1,0:T(8,128)S(1)}, f32[1024,256]{1,0:T(8,128)S(1)}, bf16[1024,192]{1,0:T(8,128)(2,1)S(1)}, f32[64,256]{1,0:T(8,128)S(1)}) custom-call(f32[1024,256]{1,0:T(8,128)} %bitcast.11, f32[1024,1024]{1,0:T(8,128)} %bitcast.9, f32[1024,1024]{1,0:T(8,128)} %bitcast.10, f32[64,1024]{1,0:T(8,128)} %bitcast.12, f32[1,64]{1,0:T(1,128)} %bitcast.14, ...), custom_call_target="tpu_custom_call" | custom-call | tf_op jit(solution)/shard_map/pallas_call | solution.py:655
  44.3 2.2 %shard_map.87 = (f32[1024,256]{1,0:T(8,128)}, f32[1024,256]{1,0:T(8,128)}) custom-call(f32[1024,256]{1,0:T(8,128)S(1)} %get-tuple-element.8.t1, f32[1024,256]{1,0:T(8,128)S(1)} %get-tuple-element.9.t2, bf16[1024,192]{1,0:T(8,128)(2,1)S(1)} %get-tuple-element.10.thin, f32[64,256]{1,0:T(8,128)S(1)} %get-tuple-element.11.chain), custom_call_target="tpu_custom_call" | custom-call | tf_op jit(solution)/shard_map/pallas_call | solution.py:728

commit v3 on v2

--- a/solution.py
+++ b/solution.py
@@ -8,9 +8,9 @@
 from jax.sharding import PartitionSpec as P
 
 STEPS = 2
-CUTS = (0, 2, 4, 4)
-UP_CUTS = (0, 1, 4, 4)
-DOWN_CUTS = (0, 4, 4, 4)
+CUTS = (0, 4, 8, 8)
+UP_CUTS = (0, 3, 8, 8)
+DOWN_CUTS = (0, 8, 8, 8)
 MESH = pl.DeviceIdType.MESH
 F32 = jnp.float32
 BF16 = jnp.bfloat16
@@ -76,7 +76,7 @@
     t1_ref, t2_ref, thin_ref, last_ref,
     n_buf, d_buf, nh, nl, dh, dl, perm, perm_t,
     r_buf, jump, high_v, low_v, high_w, low_w, fsend, frecv, fix, c_all, cs, psend, gath, qsend, cown, cprev, csend,
-    sel, npp, base, decay_v, rows_v, prim_v, esend, erecv, edges, chain_v, hsend, hrecv,
+    sel, npp, base, decay_v, rows_v, prim_v, esend, erecv, edges, couple, chain_v, hsend, hrecv,
     load_sem, small_sem, cf_ssem, cp_ssem, c_rsem, f_ssem, f_rsem, a_ssem, g_rsem,
     q_ssem, q_rsem, p_ssem, p_rsem, e_ssem, e_rsem, h_ssem, h_rsem, line_sem,
 ):
@@ -198,6 +198,8 @@
             [x[:, j * columns : (j + 1) * columns] for j in range(x.shape[1] // columns)], axis=0
         )
 
+    apart = pl.when(a >= 0)
+
     def rows_of(i, size):
         if isinstance(i, int):
             return pl.ds(i * size, size)
@@ -221,7 +223,7 @@
 
     def face_part(step, link, first, stop):
         _, where, here, there, _ = link
-        size = face // 4
+        size = face // 8
 
         def part_of(slot):
             start = slot * face + first * size
@@ -287,10 +289,12 @@
             ).astype(BF16)
 
     def take_faces(step, field, some):
-        for slot in some:
-            at = slice(slot * face, (slot + 1) * face)
-            picks = perm[at, :]
-            fsend[step, at, :] = dot(picks, field[0]) + dot(picks, field[1])
+        for link in some:
+
+            @apart
+            def _(at=rows_of(link[2], face)):
+                picks = perm[at, :]
+                fsend[step, at, :] = dot(picks, field[0]) + dot(picks, field[1])
 
     smalls[0].wait()
     for slot in range(slots):
@@ -299,11 +303,11 @@
     for load in loads[1:]:
         load.start()
     field = split(r_buf[...])
-    take_faces(0, field, range(xs, slots))
+    take_faces(0, field, links[:1])
     pl.semaphore_wait(barrier, count)
     when(links[0][0], face_copy(0, links[0]).start)
-    take_faces(0, field, range(xs))
     for link in links[1:]:
+        take_faces(0, field, [link])
         when(link[0], face_copy(0, link).start)
     if nz > 1:
         line_round(0)
@@ -418,59 +422,119 @@
         return remote(
             psend.at[step, mate_at[d]],
             gath.at[step, me],
-            a_ssem.at[step, dz, d],
-            g_rsem.at[step, me],
+            a_ssem.at[step],
+            g_rsem.at[step],
             a,
             member((team + dz) % nz, mate_at[d]),
         )
 
-    def arrived(step, who):
-        remote(
-            psend.at[step, 0], gath.at[step, who], a_ssem.at[step, 0, 0], g_rsem.at[step, who],
-            a, partner,
-        ).wait_recv()
+    def all_spread(step):
+        every = gath.at[step, pl.ds(0, ny_all - 1)]
+        return remote(every, every, a_ssem.at[step], g_rsem.at[step], a, partner)
 
     def q_copy(step, d):
         return remote(
-            qsend.at[step, mate_at[d]], cown.at[step, g], q_ssem.at[step, d], q_rsem.at[step, g],
+            qsend.at[step, mate_at[d]], cown.at[step, g], q_ssem.at[step], q_rsem.at[step],
             a, mates[d],
         )
 
     def first_copy(step, d):
         return remote(
-            qsend.at[step, mate_at[d]], cprev.at[step, g], p_ssem.at[step, d], p_rsem.at[step, g],
+            qsend.at[step, mate_at[d]], cprev.at[step, g], p_ssem.at[step], p_rsem.at[step],
             a + 1, mates[d],
         )
 
     def next_copy(step, q):
         return remote(
-            csend.at[step, q], cprev.at[step, q], p_ssem.at[step, q], p_rsem.at[step, q],
+            csend.at[step, q], cprev.at[step, q], p_ssem.at[step], p_rsem.at[step],
             a + 1, me,
         )
+
+    def all_q(step):
+        every = cown.at[step, pl.ds(0, ng - 1)]
+        return remote(every, every, q_ssem.at[step], q_rsem.at[step], a, partner)
+
+    def all_p(step):
+        every = cprev.at[step]
+        return remote(every, every, p_ssem.at[step], p_rsem.at[step], a, partner)
 
     starts = jnp.logical_and(a == 0, a < nx - 1)
     passes = jnp.logical_and(a > 0, a < nx - 1)
 
+    def sent_later(step):
+        if step == 0:
+            coarse_near(0).wait_send()
+            for dy in range(1, ny):
+                coarse_far(dy).wait_send()
+                coarse_near(dy).wait_send()
+            for link in links:
+                when(link[0], edge_copy(link).wait_send)
+                when(link[0], face_copy(0, link).wait_send)
+        if step + 1 < STEPS:
+            for link in links:
+                when(link[0], face_copy(step + 1, link).wait_send)
+                when(both(link[0], goes_down(link)), chain_copy(step, link).wait_send)
+        all_q(step).wait_send()
+        pl.when(a < nx - 1)(all_p(step).wait_send)
+
     for step in range(STEPS):
         last = step + 1 == STEPS
-        source = r_buf if step == 0 else t2_ref
-        for link in links:
-            arrives(functools.partial(face_copy, step), link)
         if step == 0:
-            ghost = split(frecv[step])
+            arrives(functools.partial(face_copy, step), links[-1])
+            inner = pl.ds(pl.multiple_of(in_slot * face, face), face)
+            ghost = split(frecv[step, inner, :])
+
+            def start_fill(i, carry, ghost=ghost, inner=inner):
+                at = rows_of(i, block)
+                back = perm_t[at, inner]
+                jump[at, :] = r_buf[at, :] - dot(back, ghost[0]) - dot(back, ghost[1])
+                return carry
+
+            lax.fori_loop(0, blocks, start_fill, 0)
+            for link in links[:-1]:
+                arrives(functools.partial(face_copy, step), link)
+
+            @apart
+            def _(step=step):
+                base[...] -= stacked3(npp[...], split(frecv[step]))
+
+            prim = base[...]
         else:
-            ghost = split(frecv[step] - fix[...])
-        prim = base[...] - stacked3(npp[...], ghost)
+            for link in links:
+                arrives(functools.partial(face_copy, step), link)
+
+            @apart
+            def _(step=step):
+                base[...] -= stacked3(npp[...], split(frecv[step]))
+
+            for link in links:
+                arrives(functools.partial(chain_copy, step - 1), link, comes_down(link))
+            beside = jnp.concatenate([tall3(hrecv[step - 1, slot]) for slot in range(slots)])
+            prim = base[...] + dot(couple[...], beside)
         for q in range(ng):
             psend[step, q] = pack(prim[:, q * part : (q + 1) * part])
         for dz, d in order:
             spread(step, dz, d).start()
         gath[step, me] = psend[step, g]
-
-        def fill(i, carry, source=source, ghost=ghost):
+        if step == 0:
+            outer = pl.ds(pl.multiple_of(out_slot * face, face), face)
+            sides = [(pl.ds(slot * face, face)) for slot in range(xs)] + [outer]
+            ghosts = [split(frecv[step, side, :]) for side in sides]
+        else:
+            for slot in range(slots):
+                at = slice(slot * face, (slot + 1) * face)
+                fix[at, :] = frecv[step, at, :] - 0.5 * dot(
+                    edges[at, :], beside[slot * 3 * prims : (slot + 1) * 3 * prims]
+                )
+            sides = [pl.ds(0, slots * face)]
+            ghosts = [split(fix[...])]
+
+        def fill(i, carry, step=step, sides=sides, ghosts=ghosts):
             at = rows_of(i, block)
-            back = perm_t[at, :]
-            value = source[at, :] - dot(back, ghost[0]) - dot(back, ghost[1])
+            value = jump[at, :] if step == 0 else t2_ref[at, :]
+            for side, ghost in zip(sides, ghosts):
+                back = perm_t[at, side]
+                value = value - dot(back, ghost[0]) - dot(back, ghost[1])
             jump[at, :] = value
             high_v[at, :], low_v[at, :] = split(value)
             return carry
@@ -505,10 +569,10 @@
         lax.fori_loop(0, blocks, smooth, 0)
         if not last:
             rests = (high_v[...], low_v[...])
-            take_faces(step + 1, rests, range(xs, slots))
-            send_part(step + 1, 0, links[:1])
-            take_faces(step + 1, rests, range(xs))
-            send_part(step + 1, 0, links[1:-1])
+            for link in links[:-1]:
+                take_faces(step + 1, rests, [link])
+                send_part(step + 1, 0, [link])
+            take_faces(step + 1, rests, links[-1:])
             face_copy(step + 1, links[-1]).start()
         if step == 0:
             for dy in range(ny):
@@ -517,12 +581,16 @@
             cs[0:size, :], cs[size : 2 * size, :] = split(
                 c_all[...].reshape(size, c_all.shape[2])
             )
-        for dz, d in order:
-            arrived(step, member((team + dz) % nz, mate_at[d]))
-        values = jnp.concatenate([unpack(gath[step, b]) for b in range(ny_all)], axis=0)
-        quarter = stacked3(cs[...], split(values))
-        for q in range(ng):
-            qsend[step, q] = pack(quarter[q * prims : (q + 1) * prims, :])
+        if step > 0:
+            sent_later(step - 1)
+        all_spread(step).wait_recv()
+
+        @apart
+        def _(step=step):
+            values = jnp.concatenate([unpack(gath[step, b]) for b in range(ny_all)], axis=0)
+            quarter = stacked3(cs[...], split(values))
+            for q in range(ng):
+                qsend[step, q] = pack(quarter[q * prims : (q + 1) * prims, :])
 
         @pl.when(starts)
         def _(step=step):
@@ -534,11 +602,8 @@
         if not last:
             send_part(step + 1, 1, links[:-1])
         cown[step, g] = qsend[step, g]
-        for d in range(1, ng):
-            remote(
-                qsend.at[step, 0], cown.at[step, mate_at[d]], q_ssem.at[step, 0],
-                q_rsem.at[step, mate_at[d]], a, partner,
-            ).wait_recv()
+        all_spread(step).wait_send()
+        all_q(step).wait_recv()
 
         def joined(ref, step=step):
             return jnp.concatenate([unpack(ref[step, q]) for q in range(ng)], axis=1)
@@ -549,8 +614,7 @@
 
         @pl.when(a > 0)
         def _(step=step):
-            for q in range(ng):
-                next_copy(step, q).wait_recv()
+            all_p(step).wait_recv()
             chain_v[...] = joined(cown) + rate * joined(cprev)
 
         @pl.when(passes)
@@ -587,41 +651,16 @@
                 for link in links:
                     arrives(edge_copy, link)
                 for slot in range(slots):
+                    at = slice(slot * face, (slot + 1) * face)
                     high, low = split(unpack(erecv[slot], prims))
-                    edges[slot * face : (slot + 1) * face, :] = jnp.concatenate(
-                        [high, high, low], axis=1
-                    )
-            for link in links:
-                arrives(functools.partial(chain_copy, step), link, comes_down(link))
-            for slot in range(slots):
-                at = slice(slot * face, (slot + 1) * face)
-                fix[at, :] = 0.5 * dot(edges[at, :], tall3(hrecv[step, slot]))
-
-    coarse_near(0).wait_send()
-    for dy in range(1, ny):
-        coarse_far(dy).wait_send()
-        coarse_near(dy).wait_send()
-    for link in links:
-        when(link[0], edge_copy(link).wait_send)
-    for step in range(STEPS):
-        for link in links:
-            when(link[0], face_copy(step, link).wait_send)
-            if step + 1 < STEPS:
-                when(both(link[0], goes_down(link)), chain_copy(step, link).wait_send)
-        for dz, d in order:
-            spread(step, dz, d).wait_send()
-        for d in range(1, ng):
-            q_copy(step, d).wait_send()
-
-        @pl.when(starts)
-        def _(step=step):
-            for d in range(ng):
-                first_copy(step, d).wait_send()
-
-        @pl.when(passes)
-        def _(step=step):
-            for q in range(ng):
-                next_copy(step, q).wait_send()
+                    edges[at, :] = jnp.concatenate([high, high, low], axis=1)
+                    both_ways = dot(npp[:, at], edges[at, :])
+                    across = both_ways[:prims, :prims] + both_ways[:prims, 2 * prims :]
+                    high, low = split(0.5 * (across + both_ways[prims:, :prims]))
+                    for k, piece_of in enumerate((high, high, low)):
+                        left = (3 * slot + k) * prims
+                        couple[:, left : left + prims] = piece_of
+    sent_later(STEPS - 1)
 
 
 def closing(t1, t2, thin, chain, sol, res):
@@ -689,6 +728,7 @@
             pltpu.VMEM(edge, F32),
             pltpu.VMEM(edge, F32),
             pltpu.VMEM((slots * face, 3 * prims), BF16),
+            pltpu.VMEM((prims, slots * 3 * prims), BF16),
             pltpu.VMEM((prims, width), F32),
             pltpu.VMEM((STEPS - 1, prims, width), F32),
             pltpu.VMEM((STEPS - 1, slots, prims, width), F32),
@@ -699,12 +739,12 @@
             dma((ng,)),
             dma((STEPS, slots)),
             dma((STEPS, slots)),
-            dma((STEPS, nz, ng)),
-            dma((STEPS, ny_all)),
-            dma((STEPS, ng)),
-            dma((STEPS, ng)),
-            dma((STEPS, ng)),
-            dma((STEPS, ng)),
+            dma((STEPS,)),
+            dma((STEPS,)),
+            dma((STEPS,)),
+            dma((STEPS,)),
+            dma((STEPS,)),
+            dma((STEPS,)),
             dma((slots,)),
             dma((slots,)),
             dma((STEPS - 1, slots)),
@@ -723,7 +763,7 @@
         face_rows[0],
         primal[0],
     )
-    rows = unknowns // 4
+    rows = unknowns // 2
     tall = pl.BlockSpec((rows, width), lambda i: (i, 0))
     sol, res = pl.pallas_call(
         closing,

time: 46.6 us -> 43.7 us (0.938)
  Pallas kernels: 45.8 us -> 42.9 us
    pallas_call x1, Pallas kernels: 43.6 us -> 41.3 us  [local(): pl.pallas_call(functools.partial(kernel, nx, ny_all), out_shape=tuple((pl...]
    pallas_call x1, Pallas kernels: 2.17 us -> 1.57 us  [local(): pl.pallas_call(closing, grid=(unknowns // rows,), out_shape=(whole, whole...]
where the time goes in v3:
time: 43.7 us; the launch traced here: 43.5 us
  Pallas kernels  42.9 us (98%)
  between operations  0.64 us (1%)
    pallas_call x1, Pallas kernels, local(): pl.pallas_call(functools.partial(kernel, nx, ny_all), out_shape=tuple((pl...  41.3 us
    pallas_call x1, Pallas kernels, local(): pl.pallas_call(closing, grid=(unknowns // rows,), out_shape=(whole, whole...  1.57 us

profile of v3, /device:TPU:0, one launch (start us, length us, event | category | flops | bytes accessed | tf_op | source)
XLA Modules:
  0.0 43.5 jit_solution(9471107410819354577)
XLA Ops:
  0.6 41.3 %shard_map.86 = (f32[1024,256]{1,0:T(8,128)S(1)}, f32[1024,256]{1,0:T(8,128)S(1)}, bf16[1024,192]{1,0:T(8,128)(2,1)S(1)}, f32[64,256]{1,0:T(8,128)S(1)}) custom-call(f32[1024,256]{1,0:T(8,128)} %bitcast.11, f32[1024,1024]{1,0:T(8,128)} %bitcast.9, f32[1024,1024]{1,0:T(8,128)} %bitcast.10, f32[64,1024]{1,0:T(8,128)} %bitcast.12, f32[1,64]{1,0:T(1,128)} %bitcast.14, ...), custom_call_target="tpu_custom_call" | custom-call | tf_op jit(solution)/shard_map/pallas_call | solution.py:694
  42.0 1.6 %shard_map.87 = (f32[1024,256]{1,0:T(8,128)}, f32[1024,256]{1,0:T(8,128)}) custom-call(f32[1024,256]{1,0:T(8,128)S(1)} %get-tuple-element.8.t1, f32[1024,256]{1,0:T(8,128)S(1)} %get-tuple-element.9.t2, bf16[1024,192]{1,0:T(8,128)(2,1)S(1)} %get-tuple-element.10.thin, f32[64,256]{1,0:T(8,128)S(1)} %get-tuple-element.11.chain), custom_call_target="tpu_custom_call" | custom-call | tf_op jit(solution)/shard_map/pallas_call | solution.py:768

commit v4 on v3

--- a/solution.py
+++ b/solution.py
@@ -9,7 +9,7 @@
 
 STEPS = 2
 CUTS = (0, 4, 8, 8)
-UP_CUTS = (0, 3, 8, 8)
+UP_CUTS = (0, 2, 8, 8)
 DOWN_CUTS = (0, 8, 8, 8)
 MESH = pl.DeviceIdType.MESH
 F32 = jnp.float32
@@ -140,7 +140,10 @@
         links.append((a > 0, (a - 1, me), 0, 1, False))
         links.append((a < nx - 1, (a + 1, me), 1, 0, True))
     links.append((True, (a, partner), in_slot, out_slot, None))
-    mate_at = [(g + d) % ng for d in range(ng)]
+    mate_at = [
+        (z + dz) % ny * 2 + (core + dc) % 2
+        for dz, dc in [(0, 0)] + [(k, c) for k in range(1, ny) for c in range(2)] + [(0, 1)]
+    ]
     mates = [member(team, j) for j in mate_at]
     below, above = z > 0, z < nz - 1
     count = jnp.int32(ng - 1 + plane - 1)
@@ -594,7 +597,7 @@
 
         @pl.when(starts)
         def _(step=step):
-            for d in range(ng):
+            for d in [*range(1, ng), 0]:
                 first_copy(step, d).start()
 
         for d in range(1, ng):

time: 43.7 us -> 43.5 us (level)
  no operation moved by 1% of the time
where the time goes in v4:
time: 43.5 us; the launch traced here: 43.3 us
  Pallas kernels  42.7 us (98%)
  between operations  0.64 us (1%)
    pallas_call x1, Pallas kernels, local(): pl.pallas_call(functools.partial(kernel, nx, ny_all), out_shape=tuple((pl...  41.1 us
    pallas_call x1, Pallas kernels, local(): pl.pallas_call(closing, grid=(unknowns // rows,), out_shape=(whole, whole...  1.56 us

profile of v4, /device:TPU:0, one launch (start us, length us, event | category | flops | bytes accessed | tf_op | source)
XLA Modules:
  0.0 43.3 jit_solution(16399592655125891850)
XLA Ops:
  0.6 41.1 %shard_map.86 = (f32[1024,256]{1,0:T(8,128)S(1)}, f32[1024,256]{1,0:T(8,128)S(1)}, bf16[1024,192]{1,0:T(8,128)(2,1)S(1)}, f32[64,256]{1,0:T(8,128)S(1)}) custom-call(f32[1024,256]{1,0:T(8,128)} %bitcast.11, f32[1024,1024]{1,0:T(8,128)} %bitcast.9, f32[1024,1024]{1,0:T(8,128)} %bitcast.10, f32[64,1024]{1,0:T(8,128)} %bitcast.12, f32[1,64]{1,0:T(1,128)} %bitcast.14, ...), custom_call_target="tpu_custom_call" | custom-call | tf_op jit(solution)/shard_map/pallas_call | solution.py:697
  41.8 1.6 %shard_map.87 = (f32[1024,256]{1,0:T(8,128)}, f32[1024,256]{1,0:T(8,128)}) custom-call(f32[1024,256]{1,0:T(8,128)S(1)} %get-tuple-element.8.t1, f32[1024,256]{1,0:T(8,128)S(1)} %get-tuple-element.9.t2, bf16[1024,192]{1,0:T(8,128)(2,1)S(1)} %get-tuple-element.10.thin, f32[64,256]{1,0:T(8,128)S(1)} %get-tuple-element.11.chain), custom_call_target="tpu_custom_call" | custom-call | tf_op jit(solution)/shard_map/pallas_call | solution.py:771

commit v5 on v4

--- a/solution.py
+++ b/solution.py
@@ -10,7 +10,7 @@
 STEPS = 2
 CUTS = (0, 4, 8, 8)
 UP_CUTS = (0, 2, 8, 8)
-DOWN_CUTS = (0, 8, 8, 8)
+DOWN_CUTS = (0, 4, 8, 8)
 MESH = pl.DeviceIdType.MESH
 F32 = jnp.float32
 BF16 = jnp.bfloat16
@@ -76,9 +76,9 @@
     t1_ref, t2_ref, thin_ref, last_ref,
     n_buf, d_buf, nh, nl, dh, dl, perm, perm_t,
     r_buf, jump, high_v, low_v, high_w, low_w, fsend, frecv, fix, c_all, cs, psend, gath, qsend, cown, cprev, csend,
-    sel, npp, base, decay_v, rows_v, prim_v, esend, erecv, edges, couple, chain_v, hsend, hrecv,
+    sel, npp, base, decay_v, rows_v, prim_v, esend, erecv, edges, couple, chain_v, hsend, hrecv, cup, rate_out, rate_in,
     load_sem, small_sem, cf_ssem, cp_ssem, c_rsem, f_ssem, f_rsem, a_ssem, g_rsem,
-    q_ssem, q_rsem, p_ssem, p_rsem, e_ssem, e_rsem, h_ssem, h_rsem, line_sem,
+    q_ssem, q_rsem, p_ssem, p_rsem, e_ssem, e_rsem, h_ssem, h_rsem, u_ssem, u_rsem, rate_sem, line_sem,
 ):
     unknowns, width = r_buf.shape
     face = unknowns // 4
@@ -157,14 +157,15 @@
     pl.when(below)(functools.partial(greet, a, me - plane))
     pl.when(above)(functools.partial(greet, a, me + plane))
     count = count + below.astype(jnp.int32) + above.astype(jnp.int32)
-    if nx > 1:
-
-        @pl.when(a < 2)
-        def _():
-            for d in range(1, ng):
-                greet(1 - a, mates[d])
-
-        count = count + (a < 2).astype(jnp.int32) * (ng - 1)
+    for has, there in ((a > 0, a - 1), (a < nx - 1, a + 1)):
+        if nx > 1:
+
+            @pl.when(has)
+            def _(there=there):
+                for d in range(1, ng):
+                    greet(there, mates[d])
+
+            count = count + has.astype(jnp.int32) * (ng - 1)
 
     def line_round(turn):
         def tell(low):
@@ -267,12 +268,6 @@
     def arrives(copy, link, cond=True):
         has, where, here, _, up = link
         when(both(has, cond), copy((has, where, here, here, up)).wait_recv)
-
-    def comes_down(link):
-        return True if link[4] is None else link[4]
-
-    def goes_down(link):
-        return True if link[4] is None else negate(link[4])
 
     lanes = 128
 
@@ -368,6 +363,15 @@
     )
     prim_row = prim_v[...].astype(F32)
     prim_col = jnp.sum(jnp.where(eye, prim_row, 0.0), axis=1, keepdims=True)
+    rate_out[...] = jnp.broadcast_to(
+        jnp.concatenate([decay_v[...]] * (128 // prims), axis=1), rate_out.shape
+    )
+
+    def rate_copy():
+        return remote(rate_out, rate_in, rate_sem.at[0], rate_sem.at[1], a - 1, me)
+
+    if nx > 1:
+        pl.when(a > 0)(rate_copy().start)
     rate = jnp.sum(jnp.where(eye, decay_v[...], 0.0), axis=1, keepdims=True)
     pick_t = jnp.where(
         prim_col == lax.broadcasted_iota(jnp.int32, (prims, unknowns), 1).astype(F32), 1.0, 0.0
@@ -457,6 +461,16 @@
         every = cown.at[step, pl.ds(0, ng - 1)]
         return remote(every, every, q_ssem.at[step], q_rsem.at[step], a, partner)
 
+    def down_copy(step, d):
+        return remote(
+            qsend.at[step, mate_at[d]], cup.at[step, g], u_ssem.at[step], u_rsem.at[step],
+            a - 1, mates[d],
+        )
+
+    def all_u(step):
+        every = cup.at[step]
+        return remote(every, every, u_ssem.at[step], u_rsem.at[step], a, partner)
+
     def all_p(step):
         every = cprev.at[step]
         return remote(every, every, p_ssem.at[step], p_rsem.at[step], a, partner)
@@ -466,6 +480,8 @@
 
     def sent_later(step):
         if step == 0:
+            if nx > 1:
+                pl.when(a > 0)(rate_copy().wait_send)
             coarse_near(0).wait_send()
             for dy in range(1, ny):
                 coarse_far(dy).wait_send()
@@ -476,7 +492,10 @@
         if step + 1 < STEPS:
             for link in links:
                 when(link[0], face_copy(step + 1, link).wait_send)
-                when(both(link[0], goes_down(link)), chain_copy(step, link).wait_send)
+                if link[4] is None:
+                    when(link[0], chain_copy(step, link).wait_send)
+            if nx > 1:
+                pl.when(a > 0)(all_u(step).wait_send)
         all_q(step).wait_send()
         pl.when(a < nx - 1)(all_p(step).wait_send)
 
@@ -511,7 +530,8 @@
                 base[...] -= stacked3(npp[...], split(frecv[step]))
 
             for link in links:
-                arrives(functools.partial(chain_copy, step - 1), link, comes_down(link))
+                if link[4] is None:
+                    arrives(functools.partial(chain_copy, step - 1), link)
             beside = jnp.concatenate([tall3(hrecv[step - 1, slot]) for slot in range(slots)])
             prim = base[...] + dot(couple[...], beside)
         for q in range(ng):
@@ -602,6 +622,13 @@
 
         for d in range(1, ng):
             q_copy(step, d).start()
+        if nx > 1 and not last:
+
+            @pl.when(a > 0)
+            def _(step=step):
+                for d in [*range(1, ng), 0]:
+                    down_copy(step, d).start()
+
         if not last:
             send_part(step + 1, 1, links[:-1])
         cown[step, g] = qsend[step, g]
@@ -611,35 +638,30 @@
         def joined(ref, step=step):
             return jnp.concatenate([unpack(ref[step, q]) for q in range(ng)], axis=1)
 
+        chain_out = last_ref if last else hsend.at[step]
+
         @pl.when(a == 0)
-        def _(step=step):
+        def _(chain_out=chain_out):
+            chain_out[...] = joined(cown)
+
+        @pl.when(a > 0)
+        def _(step=step, chain_out=chain_out):
             chain_v[...] = joined(cown)
-
-        @pl.when(a > 0)
-        def _(step=step):
             all_p(step).wait_recv()
-            chain_v[...] = joined(cown) + rate * joined(cprev)
+            chain_out[...] = chain_v[...] + rate * joined(cprev)
 
         @pl.when(passes)
-        def _(step=step):
+        def _(step=step, chain_out=chain_out):
             for q in range(ng):
-                csend[step, q] = pack(chain_v[:, q * part : (q + 1) * part])
+                csend[step, q] = pack(chain_out[:, q * part : (q + 1) * part])
                 next_copy(step, q).start()
 
-        if last:
-            last_ref[...] = chain_v[...]
-        else:
-            hsend[step] = chain_v[...]
+        if not last:
             for link in links:
-                when(both(link[0], goes_down(link)), chain_copy(step, link).start)
+                if link[4] is None:
+                    when(link[0], chain_copy(step, link).start)
             send_part(step + 1, 2, links[:-1])
-            if nx > 1:
-
-                @pl.when(a > 0)
-                def _(step=step):
-                    hrecv[step, 0] = joined(cprev)
-
-            chain = tall3(chain_v[...])
+            chain = tall3(hsend[step])
 
             def finish(i, carry, chain=chain):
                 at = rows_of(i, block)
@@ -650,6 +672,20 @@
 
             lax.fori_loop(0, blocks, finish, 0)
             base[...] = stacked3(sel[...], split(t2_ref[...]))
+            if nx > 1:
+
+                @pl.when(a > 0)
+                def _(step=step):
+                    hrecv[step, 0] = joined(cprev)
+
+                @pl.when(a < nx - 1)
+                def _(step=step):
+                    if step == 0:
+                        rate_copy().wait_recv()
+                    all_u(step).wait_recv()
+                    above_row = rate_in[0:1, :prims]
+                    rate_up = jnp.sum(jnp.where(eye, above_row, 0.0), axis=1, keepdims=True)
+                    hrecv[step, xs - 1] = joined(cup) + rate_up * hsend[step]
             if step == 0:
                 for link in links:
                     arrives(edge_copy, link)
@@ -735,6 +771,9 @@
             pltpu.VMEM((prims, width), F32),
             pltpu.VMEM((STEPS - 1, prims, width), F32),
             pltpu.VMEM((STEPS - 1, slots, prims, width), F32),
+            pltpu.VMEM((STEPS - 1, ng) + piece, F32),
+            pltpu.VMEM((8, 128), F32),
+            pltpu.VMEM((8, 128), F32),
             dma((4,)),
             dma((3,)),
             dma((ny,)),
@@ -752,6 +791,9 @@
             dma((slots,)),
             dma((STEPS - 1, slots)),
             dma((STEPS - 1, slots)),
+            dma((STEPS - 1,)),
+            dma((STEPS - 1,)),
+            dma((2,)),
             pltpu.SemaphoreType.REGULAR((max(1, nz - 1), 2)),
         ],
         compiler_params=pltpu.CompilerParams(

time: 43.5 us -> 43.5 us (level)
  no operation moved by 1% of the time
where the time goes in v5:
time: 43.5 us; the launch traced here: 43.3 us
  Pallas kernels  42.6 us (98%)
  between operations  0.64 us (1%)
    pallas_call x1, Pallas kernels, local(): pl.pallas_call(functools.partial(kernel, nx, ny_all), out_shape=tuple((pl...  41.1 us
    pallas_call x1, Pallas kernels, local(): pl.pallas_call(closing, grid=(unknowns // rows,), out_shape=(whole, whole...  1.56 us

profile of v5, /device:TPU:0, one launch (start us, length us, event | category | flops | bytes accessed | tf_op | source)
XLA Modules:
  0.0 43.3 jit_solution(3169214380132639837)
XLA Ops:
  0.6 41.1 %shard_map.86 = (f32[1024,256]{1,0:T(8,128)S(1)}, f32[1024,256]{1,0:T(8,128)S(1)}, bf16[1024,192]{1,0:T(8,128)(2,1)S(1)}, f32[64,256]{1,0:T(8,128)S(1)}) custom-call(f32[1024,256]{1,0:T(8,128)} %bitcast.11, f32[1024,1024]{1,0:T(8,128)} %bitcast.9, f32[1024,1024]{1,0:T(8,128)} %bitcast.10, f32[64,1024]{1,0:T(8,128)} %bitcast.12, f32[1,64]{1,0:T(1,128)} %bitcast.14, ...), custom_call_target="tpu_custom_call" | custom-call | tf_op jit(solution)/shard_map/pallas_call | solution.py:733
  41.7 1.6 %shard_map.87 = (f32[1024,256]{1,0:T(8,128)}, f32[1024,256]{1,0:T(8,128)}) custom-call(f32[1024,256]{1,0:T(8,128)S(1)} %get-tuple-element.8.t1, f32[1024,256]{1,0:T(8,128)S(1)} %get-tuple-element.9.t2, bf16[1024,192]{1,0:T(8,128)(2,1)S(1)} %get-tuple-element.10.thin, f32[64,256]{1,0:T(8,128)S(1)} %get-tuple-element.11.chain), custom_call_target="tpu_custom_call" | custom-call | tf_op jit(solution)/shard_map/pallas_call | solution.py:813

commit v6 on v5

--- a/solution.py
+++ b/solution.py
@@ -611,7 +611,9 @@
         @apart
         def _(step=step):
             values = jnp.concatenate([unpack(gath[step, b]) for b in range(ny_all)], axis=0)
-            quarter = stacked3(cs[...], split(values))
+            size = ng * prims
+            terms = dot(cs[...], jnp.concatenate(split(values), axis=1))
+            quarter = terms[:size, :part] + terms[size:, :part] + terms[:size, part:]
             for q in range(ng):
                 qsend[step, q] = pack(quarter[q * prims : (q + 1) * prims, :])
 

time: 43.5 us -> 43.2 us (level)
  no operation moved by 1% of the time
where the time goes in v6:
time: 43.2 us; the launch traced here: 43 us
  Pallas kernels  42.4 us (98%)
  between operations  0.64 us (1%)
    pallas_call x1, Pallas kernels, local(): pl.pallas_call(functools.partial(kernel, nx, ny_all), out_shape=tuple((pl...  40.8 us
    pallas_call x1, Pallas kernels, local(): pl.pallas_call(closing, grid=(unknowns // rows,), out_shape=(whole, whole...  1.56 us

profile of v6, /device:TPU:0, one launch (start us, length us, event | category | flops | bytes accessed | tf_op | source)
XLA Modules:
  0.0 43.0 jit_solution(1545053381447310338)
XLA Ops:
  0.6 40.8 %shard_map.86 = (f32[1024,256]{1,0:T(8,128)S(1)}, f32[1024,256]{1,0:T(8,128)S(1)}, bf16[1024,192]{1,0:T(8,128)(2,1)S(1)}, f32[64,256]{1,0:T(8,128)S(1)}) custom-call(f32[1024,256]{1,0:T(8,128)} %bitcast.11, f32[1024,1024]{1,0:T(8,128)} %bitcast.9, f32[1024,1024]{1,0:T(8,128)} %bitcast.10, f32[64,1024]{1,0:T(8,128)} %bitcast.12, f32[1,64]{1,0:T(1,128)} %bitcast.14, ...), custom_call_target="tpu_custom_call" | custom-call | tf_op jit(solution)/shard_map/pallas_call | solution.py:735
  41.4 1.6 %shard_map.87 = (f32[1024,256]{1,0:T(8,128)}, f32[1024,256]{1,0:T(8,128)}) custom-call(f32[1024,256]{1,0:T(8,128)S(1)} %get-tuple-element.8.t1, f32[1024,256]{1,0:T(8,128)S(1)} %get-tuple-element.9.t2, bf16[1024,192]{1,0:T(8,128)(2,1)S(1)} %get-tuple-element.10.thin, f32[64,256]{1,0:T(8,128)S(1)} %get-tuple-element.11.chain), custom_call_target="tpu_custom_call" | custom-call | tf_op jit(solution)/shard_map/pallas_call | solution.py:815
